TPU v7x, 512 devices: a whole 4x4x16 slice. The times are simulated.
512 devices in a mesh: freq: 32 (over z_lo, x), src: 2 (over z_hi), rcv: 8 (over y, core).
Axes of the slice: x: 4, y: 4, z: 16 (z_hi: 2, z_lo: 8; z = z_hi * 8 + z_lo), core: 2. Of those that a mesh axis runs over, the one named last changes fastest.
Arguments:
- traces: float32 [1024, 1024, 256], P(('src', 'freq'), 'rcv'), may hold values from -6 to 6
Outputs:
- multiples: float32 [2, 96, 1024, 1024], P(None, 'freq', 'src', 'rcv')
All inputs are finite; a program needn't handle non-finite values.
Results may differ from a plain program's by a relative error of at most 0.000098.
Values sent between devices are 32-bit elements; how exact they have to be, the bound alone decides.
A program may use at most 64 MiB of HBM per device.

v0:
```python
import math
import jax
import jax.numpy as jnp
from jax import lax
from jax.sharding import PartitionSpec as P

N = 1024
FPD = 3


def dft_matrix(n_time, n_freq):
    times = jnp.arange(n_time, dtype=jnp.int32)
    bins = jnp.arange(n_freq, dtype=jnp.int32)
    phase = times[:, None] * bins[None, :] % n_time
    angle = phase.astype(jnp.float32) * (2.0 * math.pi / n_time)
    both = jnp.stack([jnp.cos(angle), -jnp.sin(angle)], axis=-1)
    return both.reshape(n_time, 2 * n_freq) * (1.0 / math.sqrt(n_time))


def batched_dot(left, right):
    return jnp.einsum(
        "mgq,mqn->mgn",
        left,
        right,
        precision=lax.Precision.HIGHEST,
        preferred_element_type=jnp.float32,
    )


def complex_product(left_re, left_im, right_re, right_im):
    real_part = batched_dot(left_re, right_re) - batched_dot(left_im, right_im)
    imag_part = batched_dot(left_re, right_im) + batched_dot(left_im, right_re)
    return (real_part, imag_part)


def per_device(traces):
    n_time = traces.shape[2]
    n_freq = FPD * lax.axis_size("freq")
    dft_table = dft_matrix(n_time, n_freq)
    spectra = jnp.einsum(
        "srt,tk->ksr",
        traces,
        dft_table,
        precision=lax.Precision.HIGHEST,
        preferred_element_type=jnp.float32,
    )
    regrouped = lax.all_to_all(spectra, "freq", split_axis=0, concat_axis=1, tiled=True)
    src_rows = regrouped.shape[1]
    rcv_cols = regrouped.shape[2]
    split_parts = regrouped.reshape(FPD, 2, src_rows, rcv_cols)
    local_re = split_parts[:, 0]
    local_im = split_parts[:, 1]
    col_re, col_im = (
        lax.all_gather(local_re, "src", axis=1, tiled=True),
        lax.all_gather(local_im, "src", axis=1, tiled=True),
    )
    piece_re = lax.all_gather(local_re, "rcv", axis=2, tiled=True)
    piece_im = lax.all_gather(local_im, "rcv", axis=2, tiled=True)
    real_part, imag_part = complex_product(piece_re, piece_im, col_re, col_im)
    scale = -1.0 / math.sqrt(N)
    return jnp.stack([real_part, imag_part]) * scale


def solution(mesh):
    in_specs = (P(("src", "freq"), "rcv", None),)
    out_specs = P(None, "freq", "src", "rcv")
    return jax.shard_map(
        per_device, mesh=mesh, in_specs=in_specs, out_specs=out_specs, check_vma=False
    )
```

profile of v0, /device:TPU:1, one launch (start us, length us, event | category | flops | bytes accessed | tf_op | source)
XLA Modules:
  0.0 411.7 jit_solution(3908307167513742405)
XLA Ops:
  6.5 0.0 copy-start
  6.5 0.0 all-gather.11.cloned.1.call-start
  6.5 0.4 sine_negate_fusion
  7.0 0.2 copy.14
  7.1 0.1 reshape.83
  7.3 0.8 copy-done
  8.1 2.3 fusion.39
  10.4 0.9 copy.15
  11.3 89.4 %all_to_all.15 = f32[192,16,128]{2,1,0:T(8,128)S(1)} all-to-all(f32[192,16,128]{2,1,0:T(8,128)S(1)} %copy.15), channel_id=1, replica_groups=mesh['freq'=32,'src'=2,'rcv'=8] {'freq'}, dimensions={0} | all-to-all | bytes 3145728 | tf_op jit(solution)/shard_map/all_to_all | solution.py:47
  100.7 0.1 copy.16
  100.9 1.3 slice_bitcast_fusion.1
  102.1 0.0 all-gather.11.cloned.1.call-update
  102.1 0.0 all-gather.13.cloned.1.call-start
  102.2 0.7 all-gather.13.cloned.1.call-update
  102.9 0.0 all-gather.15.cloned.1.call-start
  102.9 0.7 all-gather.15.cloned.1.call-update
  103.6 0.2 all-gather.9.cloned.1.call-start
  103.9 0.3 all-gather.9.cloned.1.call-update
  104.2 90.4 %all-gather.11.cloned.1.call-done = f32[3,1,1024,128]{3,2,0,1:T(8,128)} async-done(((f32[3,1,512,128]{3,2,0,1:T(8,128)}), f32[3,1,1024,128]{3,2,0,1:T(8,128)}) %all-gather.11.cloned.1.call-update) | async-done | bytes 1572880 | tf_op jit(solution)/shard_map/all_gather | solution.py:54
  194.6 48.8 %all-gather.13.cloned.1.call-done = f32[3,1,512,1024]{3,2,0,1:T(8,128)} async-done(((f32[3,1,512,128]{3,2,0,1:T(8,128)}), f32[3,1,512,1024]{3,2,0,1:T(8,128)}) %all-gather.13.cloned.1.call-update) | async-done | bytes 6291472 | tf_op jit(solution)/shard_map/all_gather | solution.py:58
  243.4 7.9 %fusion = f32[3,512,128]{2,1,0:T(8,128)S(1)} fusion(f32[3,1,512,1024]{3,2,0,1:T(8,128)} %all-gather.13.cloned.1.call-done, f32[3,1,1024,128]{3,2,0,1:T(8,128)} %all-gather.11.cloned.1.call-done), kind=kOutput, calls=%fused_computation | convolution fusion | flops 2415919104 | bytes 8650752 | tf_op jit(solution)/shard_map/mgq,mqn->mgn/dot_general | solution.py:21
  251.3 90.1 %all-gather.15.cloned.1.call-done = f32[3,1,1024,128]{3,2,0,1:T(8,128)} async-done(((f32[3,1,512,128]{3,2,0,1:T(8,128)}), f32[3,1,1024,128]{3,2,0,1:T(8,128)}) %all-gather.15.cloned.1.call-update) | async-done | bytes 1572880 | tf_op jit(solution)/shard_map/all_gather | solution.py:55
  341.4 8.8 %fusion.2 = f32[3,512,128]{2,1,0:T(8,128)} fusion(f32[3,1,512,1024]{3,2,0,1:T(8,128)} %all-gather.13.cloned.1.call-done, f32[3,1,1024,128]{3,2,0,1:T(8,128)} %all-gather.15.cloned.1.call-done), kind=kOutput, calls=%fused_computation.2 | convolution fusion | flops 2415919104 | bytes 8650752 | tf_op jit(solution)/shard_map/mgq,mqn->mgn/dot_general | solution.py:21
  350.2 39.8 %all-gather.9.cloned.1.call-done = f32[3,1,512,1024]{3,2,0,1:T(8,128)} async-done(((f32[3,1,512,128]{3,2,0,1:T(8,128)}), f32[3,1,512,1024]{3,2,0,1:T(8,128)}) %all-gather.9.cloned.1.call-update) | async-done | bytes 6291472 | tf_op jit(solution)/shard_map/all_gather | solution.py:57
  390.1 0.0 copy-start.1
  390.1 0.0 copy-start.2
  390.1 8.4 %fusion.22 = f32[1,3,512,128]{3,2,1,0:T(8,128)S(1)} fusion(f32[3,512,128]{2,1,0:T(8,128)S(1)} %fusion, f32[3,1,1024,128]{3,2,0,1:T(8,128)} %all-gather.15.cloned.1.call-done, f32[3,1,512,1024]{3,2,0,1:T(8,128)} %all-gather.9.cloned.1.call-done), kind=kOutput, calls=%fused_computation.15 | convolution fusion | flops 2416115712 | bytes 9437184 | tf_op jit(solution)/shard_map/mgq,mqn->mgn/dot_general | solution.py:21
  398.5 0.0 copy-done.1
  398.5 0.0 copy-done.2
  398.5 0.0 copy-done.3
  398.5 5.4 %fusion.27 = f32[1,3,512,128]{3,2,1,0:T(8,128)S(1)} fusion(f32[3,512,128]{2,1,0:T(8,128)S(1)} %copy-done.3, f32[3,1,1024,128]{3,2,0,1:T(8,128)S(1)} %copy-done.2, f32[3,1,512,1024]{3,2,0,1:T(8,128)S(1)} %copy-done.1), kind=kOutput, calls=%fused_computation.16 | convolution fusion | flops 2416115712 | bytes 9437184 | tf_op jit(solution)/shard_map/mgq,mqn->mgn/dot_general | solution.py:21
  403.9 1.2 maximum_multiply_fusion
  (2 shorter events, 0.0 us)
Async XLA Ops:
  6.5 1.6 copy-start
  6.5 188.0 %all-gather.11.cloned.1.call-start = ((), (), s32[]{:S(2)}) async-start(), calls=%async_computation.2 | async-start | bytes 2359296 | tf_op jit(solution)/shard_map/all_gather | solution.py:54
  102.1 141.2 %all-gather.13.cloned.1.call-start = ((), (), s32[]{:S(2)}) async-start(), calls=%async_computation.3 | async-start | bytes 7077888 | tf_op jit(solution)/shard_map/all_gather | solution.py:58
  102.9 238.5 %all-gather.15.cloned.1.call-start = ((), (), s32[]{:S(2)}) async-start(), calls=%async_computation.4 | async-start | bytes 2359296 | tf_op jit(solution)/shard_map/all_gather | solution.py:55
  103.6 286.5 %all-gather.9.cloned.1.call-start = ((), (), s32[]{:S(2)}) async-start(), calls=%async_computation.1 | async-start | bytes 7077888 | tf_op jit(solution)/shard_map/all_gather | solution.py:57
  390.1 8.4 %copy-start.1 = (f32[3,1,512,1024]{3,2,0,1:T(8,128)S(1)}, f32[3,1,512,1024]{3,2,0,1:T(8,128)}, u32[]{:S(2)}) copy-start(f32[3,1,512,1024]{3,2,0,1:T(8,128)} %all-gather.9.cloned.1.call-done) | copy-start | bytes 18874372
  390.1 8.4 %copy-start.2 = (f32[3,1,1024,128]{3,2,0,1:T(8,128)S(1)}, f32[3,1,1024,128]{3,2,0,1:T(8,128)}, u32[]{:S(2)}) copy-start(f32[3,1,1024,128]{3,2,0,1:T(8,128)} %all-gather.11.cloned.1.call-done) | copy-start | bytes 4718596
  390.1 8.4 %copy-start.3 = (f32[3,512,128]{2,1,0:T(8,128)S(1)}, f32[3,512,128]{2,1,0:T(8,128)}, u32[]{:S(2)}) copy-start(f32[3,512,128]{2,1,0:T(8,128)} %fusion.2) | copy-start | bytes 2359300
Sparse Core Ops, SparseCore 0:
  102.3 92.2 all-gather.10
  196.7 46.6 all-gather.12
  245.5 95.8 all-gather.14
  343.4 46.6 all-gather.8
where the time goes:
time: 412 us
  waiting for transfers between devices  271 us (66%)
  blocking collectives  89.4 us (22%)
  matrix products  32.8 us (8%)
  between operations  13.2 us (3%)
    all_gather x1, waiting for transfers between devices, per_device(): lax.all_gather(local_re, 'src', axis=1, tiled=True)  90.4 us
    all_gather x1, waiting for transfers between devices, per_device(): lax.all_gather(local_im, 'src', axis=1, tiled=True)  90.1 us
    all_to_all x1, blocking collectives, per_device(): lax.all_to_all(spectra, 'freq', split_axis=0, concat_axis=1, tiled=True)  89.4 us
    all_gather x1, waiting for transfers between devices, per_device(): piece_im = lax.all_gather(local_im, 'rcv', axis=2, tiled=True)  48.8 us
    all_gather x1, waiting for transfers between devices, per_device(): piece_re = lax.all_gather(local_re, 'rcv', axis=2, tiled=True)  39.8 us
    dot_general x4, matrix products, batched_dot(): jnp.einsum('mgq,mqn->mgn', left, right, precision=lax.Precision.HIGHEST,...  30.5 us
  transfers between devices with their start and end apart: 4, of which 4 were waited for; matrix products, arithmetic and copies ran while one was open for 4% of the time, Pallas kernels for 0%

commit v1 on v0

--- a/solution.py
+++ b/solution.py
@@ -50,8 +50,11 @@
     split_parts = regrouped.reshape(FPD, 2, src_rows, rcv_cols)
     local_re = split_parts[:, 0]
     local_im = split_parts[:, 1]
+    hold_yards = lambda u, across: jnp.concatenate(
+        lax.all_to_all(jnp.stack([u for _ in range(lax.psum(1, across))], axis=0), across, 0, 0), 1
+    )
     col_re, col_im = (
-        lax.all_gather(local_re, "src", axis=1, tiled=True),
+        hold_yards(local_re, across="src"),
         lax.all_gather(local_im, "src", axis=1, tiled=True),
     )
     piece_re = lax.all_gather(local_re, "rcv", axis=2, tiled=True)

time: 412 us -> 381 us (0.925)
  waiting for transfers between devices: 271 us -> 179 us
  blocking collectives: 89.4 us -> 151 us
    all_gather x1 -> x0, waiting for transfers between devices: 90.4 us -> none  [per_device(): lax.all_gather(local_re, 'src', axis=1, tiled=True)]
    all_to_all x0 -> x1, blocking collectives: none -> 61.6 us  [per_device(): lax.all_to_all(jnp.stack([u for _ in range(lax.psum(1, across))], axis=0)...]
  transfers between devices with their start and end apart: 4 -> 3, of which waited for: 4 -> 3; matrix products, arithmetic and copies ran while one was open for 4% -> 4% of each run, Pallas kernels for 0% -> 0%
where the time goes in v1:
time: 381 us
  waiting for transfers between devices  179 us (47%)
  blocking collectives  151 us (40%)
  matrix products  30.5 us (8%)
  between operations  13.2 us (3%)
  local copies, waits for them, and re-layouts  4.79 us (1%)
    all_to_all x1, blocking collectives, per_device(): lax.all_to_all(spectra, 'freq', split_axis=0, concat_axis=1, tiled=True)  89.4 us
    all_gather x1, waiting for transfers between devices, per_device(): lax.all_gather(local_im, 'src', axis=1, tiled=True)  86.5 us
    all_to_all x1, blocking collectives, per_device(): lax.all_to_all(jnp.stack([u for _ in range(lax.psum(1, across))], axis=0)...  61.6 us
    all_gather x1, waiting for transfers between devices, per_device(): piece_im = lax.all_gather(local_im, 'rcv', axis=2, tiled=True)  50.6 us
    all_gather x1, waiting for transfers between devices, per_device(): piece_re = lax.all_gather(local_re, 'rcv', axis=2, tiled=True)  40.9 us
    dot_general x4, matrix products, batched_dot(): jnp.einsum('mgq,mqn->mgn', left, right, precision=lax.Precision.HIGHEST,...  28.2 us
  transfers between devices with their start and end apart: 3, of which 3 were waited for; matrix products, arithmetic and copies ran while one was open for 4% of the time, Pallas kernels for 0%

profile of v1, /device:TPU:1, one launch (start us, length us, event | category | flops | bytes accessed | tf_op | source)
XLA Modules:
  0.0 380.7 jit_solution(12958866766050635829)
XLA Ops:
  6.5 0.0 copy-start
  6.5 0.0 all-gather.11.cloned.1.call-start
  6.5 0.4 sine_negate_fusion
  7.0 0.2 copy.18
  7.1 0.1 reshape.90
  7.3 0.8 copy-done
  8.1 2.3 fusion.33
  10.4 0.9 copy.19
  11.3 89.4 %all_to_all.20 = f32[192,16,128]{2,1,0:T(8,128)S(1)} all-to-all(f32[192,16,128]{2,1,0:T(8,128)S(1)} %copy.19), channel_id=1, replica_groups=mesh['freq'=32,'src'=2,'rcv'=8] {'freq'}, dimensions={0} | all-to-all | bytes 3145728 | tf_op jit(solution)/shard_map/all_to_all | solution.py:47
  100.7 0.1 copy.20
  100.8 1.3 slice_bitcast_fusion.2
  102.2 0.0 all-gather.11.cloned.1.call-update
  102.2 0.0 all-gather.9.cloned.1.call-start
  102.2 0.7 all-gather.9.cloned.1.call-update
  103.0 0.0 all-gather.7.cloned.1.call-start
  103.0 0.7 all-gather.7.cloned.1.call-update
  103.7 0.1 pad_maximum_fusion
  103.8 61.6 %all_to_all.21 = f32[2,3,512,128]{3,2,1,0:T(8,128)S(1)} all-to-all(f32[2,3,512,128]{3,2,1,0:T(8,128)S(1)} %pad_maximum_fusion), channel_id=1, replica_groups=mesh['freq'=32,'src'=2,'rcv'=8] {'src'}, dimensions={0} | all-to-all | bytes 3145728 | tf_op jit(solution)/shard_map/all_to_all | solution.py:54
  165.4 1.2 copy.22
  166.7 86.5 %all-gather.11.cloned.1.call-done = f32[3,1,1024,128]{3,2,0,1:T(8,128)} async-done(((f32[3,1,512,128]{3,2,0,1:T(8,128)}), f32[3,1,1024,128]{3,2,0,1:T(8,128)}) %all-gather.11.cloned.1.call-update) | async-done | bytes 1572880 | tf_op jit(solution)/shard_map/all_gather | solution.py:58
  253.1 50.6 %all-gather.9.cloned.1.call-done = f32[3,1,512,1024]{3,2,0,1:T(8,128)} async-done(((f32[3,1,512,128]{3,2,0,1:T(8,128)}), f32[3,1,512,1024]{3,2,0,1:T(8,128)}) %all-gather.9.cloned.1.call-update) | async-done | bytes 6291472 | tf_op jit(solution)/shard_map/all_gather | solution.py:61
  303.7 0.0 copy-start.2
  303.7 9.0 %fusion.2 = f32[3,512,128]{2,1,0:T(8,128)} fusion(f32[3,1,512,1024]{3,2,0,1:T(8,128)} %all-gather.9.cloned.1.call-done, f32[3,1,1024,128]{3,2,0,1:T(8,128)} %all-gather.11.cloned.1.call-done), kind=kOutput, calls=%fused_computation.2 | convolution fusion | flops 2415919104 | bytes 8650752 | tf_op jit(solution)/shard_map/mgq,mqn->mgn/dot_general | solution.py:21
  312.8 0.0 copy-done.2
  312.8 0.0 copy-done.3
  312.8 5.3 %fusion = f32[3,512,128]{2,1,0:T(8,128)S(1)} fusion(f32[3,1024,128]{2,1,0:T(8,128)S(1)} %bitcast.51, f32[3,1,512,1024]{3,2,0,1:T(8,128)S(1)} %copy-done.2), kind=kOutput, calls=%fused_computation | convolution fusion | flops 2415919104 | bytes 8650752 | tf_op jit(solution)/shard_map/mgq,mqn->mgn/dot_general | solution.py:21
  318.1 40.9 %all-gather.7.cloned.1.call-done = f32[3,1,512,1024]{3,2,0,1:T(8,128)} async-done(((f32[3,1,512,128]{3,2,0,1:T(8,128)}), f32[3,1,512,1024]{3,2,0,1:T(8,128)}) %all-gather.7.cloned.1.call-update) | async-done | bytes 6291472 | tf_op jit(solution)/shard_map/all_gather | solution.py:60
  359.0 8.5 %fusion.23 = f32[1,3,512,128]{3,2,1,0:T(8,128)S(1)} fusion(f32[3,512,128]{2,1,0:T(8,128)} %fusion.2, f32[3,1024,128]{2,1,0:T(8,128)} %bitcast.50, f32[3,1,512,1024]{3,2,0,1:T(8,128)} %all-gather.7.cloned.1.call-done), kind=kOutput, calls=%fused_computation.15 | convolution fusion | flops 2416115712 | bytes 9437184 | tf_op jit(solution)/shard_map/mgq,mqn->mgn/dot_general | solution.py:21
  367.5 0.0 copy-done.1
  367.5 0.0 copy-done.4
  367.5 5.4 %fusion.18 = f32[1,3,512,128]{3,2,1,0:T(8,128)S(1)} fusion(f32[3,512,128]{2,1,0:T(8,128)S(1)} %fusion, f32[3,1,1024,128]{3,2,0,1:T(8,128)S(1)} %copy-done.4, f32[3,1,512,1024]{3,2,0,1:T(8,128)S(1)} %copy-done.1), kind=kOutput, calls=%fused_computation.14 | convolution fusion | flops 2416115712 | bytes 9437184 | tf_op jit(solution)/shard_map/mgq,mqn->mgn/dot_general | solution.py:21
  372.9 1.2 maximum_multiply_fusion
  (4 shorter events, 0.0 us)
Async XLA Ops:
  6.5 1.6 copy-start
  6.5 246.6 %all-gather.11.cloned.1.call-start = ((), (), s32[]{:S(2)}) async-start(), calls=%async_computation.4 | async-start | bytes 2359296 | tf_op jit(solution)/shard_map/all_gather | solution.py:58
  102.2 201.5 %all-gather.9.cloned.1.call-start = ((), (), s32[]{:S(2)}) async-start(), calls=%async_computation.3 | async-start | bytes 7077888 | tf_op jit(solution)/shard_map/all_gather | solution.py:61
  103.0 256.1 %all-gather.7.cloned.1.call-start = ((), (), s32[]{:S(2)}) async-start(), calls=%async_computation.2 | async-start | bytes 7077888 | tf_op jit(solution)/shard_map/all_gather | solution.py:60
  303.7 9.0 %copy-start.2 = (f32[3,1,512,1024]{3,2,0,1:T(8,128)S(1)}, f32[3,1,512,1024]{3,2,0,1:T(8,128)}, u32[]{:S(2)}) copy-start(f32[3,1,512,1024]{3,2,0,1:T(8,128)} %all-gather.9.cloned.1.call-done) | copy-start | bytes 18874372
  303.7 9.0 %copy-start.3 = (f32[3,2,512,128]{3,2,1,0:T(8,128)S(1)}, f32[3,2,512,128]{3,2,1,0:T(8,128)}, u32[]{:S(2)}) copy-start(f32[3,2,512,128]{3,2,1,0:T(8,128)} %copy.22) | copy-start | bytes 4718596
  359.0 8.5 %copy-start.1 = (f32[3,1,512,1024]{3,2,0,1:T(8,128)S(1)}, f32[3,1,512,1024]{3,2,0,1:T(8,128)}, u32[]{:S(2)}) copy-start(f32[3,1,512,1024]{3,2,0,1:T(8,128)} %all-gather.7.cloned.1.call-done) | copy-start | bytes 18874372
  359.0 8.5 %copy-start.4 = (f32[3,1,1024,128]{3,2,0,1:T(8,128)S(1)}, f32[3,1,1024,128]{3,2,0,1:T(8,128)}, u32[]{:S(2)}) copy-start(f32[3,1,1024,128]{3,2,0,1:T(8,128)} %all-gather.11.cloned.1.call-done) | copy-start | bytes 4718596
Sparse Core Ops, SparseCore 0:
  102.3 150.7 all-gather.10
  255.2 48.4 all-gather.8
  305.9 53.0 all-gather.6
